TPU v7x, 32 devices: a whole 2x2x4 slice. The times are simulated.
32 devices in a mesh: seq: 16 (over z, x, core), head: 2 (over y).
Axes of the slice: x: 2, y: 2, z: 4, core: 2. Of those that a mesh axis runs over, the one named last changes fastest.
Arguments:
- points: bfloat16 [16384, 512], P(('seq', 'head')), may hold values from -5000 to 5000
- norm_gain: float32 [512], replicated, may hold values from 0.1 to 1.9
- qkv_weight: bfloat16 [3, 512, 512], replicated, may hold values from -24 to 24
- out_weight: bfloat16 [512, 512], replicated, may hold values from -4 to 4
- neighbours: int32 [64, 8], replicated, may hold values from 0 to 63, as said below
Outputs:
- update: bfloat16 [16384, 512], P(('seq', 'head'))
Inputs may be any that keep to these rules, and one draw needn't show every extreme that they name: `neighbours`: column 0 of row p is p. Columns 1 to 4 are distinct patches p + s with 0 < |s| <= 4. The last 3 columns name patches whose owner (patch // 4) is not the owner of p. Over all patches of one owner, the far columns name any one other owner at most 1 times, each time a different patch, and every owner reaches 1 with some other owner.
All inputs are finite; a program needn't handle non-finite values.
Results may differ from a plain program's by a relative error of at most 0.006.
The roundings to bfloat16 on the way count: a program that leaves them out, or rounds other values in their place, can miss the bound.
Values may be sent and summed in bfloat16 or wider, within the bound.
No kernel may reach another device: no remote copies, remote signals or barrier semaphores. Data moves between devices by JAX's collectives and lax.ppermute only.
A program may use at most 64 MiB of HBM per device.

v0:
```python
import jax
import jax.numpy as jnp
from jax import lax
from jax.sharding import PartitionSpec as P

D = 512
HEAD_DIM = 32
PATCH = 256
NEIGH = 8
NEAR = 4
FAR = 3
EPS = 1e-06


def with_halo(cells, sides, width):
    for axis, dim in sides:
        count = lax.axis_size(axis)
        ends = count - 1
        head = lax.slice_in_dim(cells, 0, width, axis=dim)
        tail = lax.slice_in_dim(cells, cells.shape[dim] - width, cells.shape[dim], axis=dim)
        cells = jnp.concatenate(
            [
                lax.ppermute(tail, axis, [(i, (i + 1) % count) for i in range(ends)]),
                cells,
                lax.ppermute(head, axis, [((i + 1) % count, i) for i in range(ends)]),
            ],
            axis=dim,
        )
    return cells


def attend_patch(operands):
    query_rows, kv_rows = operands
    local_width = query_rows.shape[1]
    local_heads = local_width // HEAD_DIM
    query_rows = query_rows.reshape(PATCH, local_heads, HEAD_DIM)
    key_rows = kv_rows[:, :local_width].reshape(-1, local_heads, HEAD_DIM)
    values = kv_rows[:, local_width:].reshape(-1, local_heads, HEAD_DIM)
    scores = jnp.einsum(
        "qhd,khd->hqk", query_rows, key_rows, preferred_element_type=jnp.float32
    ) * HEAD_DIM ** (-0.5)
    row_top = jnp.max(scores, axis=2, keepdims=True)
    lifted = jnp.exp(scores - row_top)
    weights = (lifted / jnp.sum(lifted, axis=2, keepdims=True)).astype(jnp.bfloat16)
    mixed_rows = jnp.einsum("hqk,khd->qhd", weights, values, preferred_element_type=jnp.float32)
    return mixed_rows.astype(jnp.bfloat16).reshape(PATCH, local_width)


def body(points, norm_gain, qkv_weight, out_weight, neighbours):
    head_count = lax.axis_size("head")
    head_index = lax.axis_index("head")
    seq_count = lax.axis_size("seq")
    shard_index = lax.axis_index("seq")
    column_share = D // head_count
    floats = points.astype(jnp.float32)
    mean_square = jnp.sum(floats * floats, axis=1, keepdims=True) / D
    normed = (floats * lax.rsqrt(mean_square + EPS) * norm_gain).astype(jnp.bfloat16)
    grouped_weight = (
        qkv_weight.reshape(3, D, head_count, column_share)
        .transpose(1, 2, 0, 3)
        .reshape(D, head_count, 3 * column_share)
    )
    own_columns = lax.dynamic_index_in_dim(grouped_weight, head_index, 1, keepdims=False)
    projected = jnp.dot(
        lax.all_gather(normed, "head", axis=0, tiled=True),
        own_columns,
        preferred_element_type=jnp.float32,
    ).astype(jnp.bfloat16)
    row_count = projected.shape[0]
    per_shard = row_count // PATCH
    queries = projected[:, :column_share]
    kv_local = projected[:, column_share:].reshape(per_shard, PATCH, 2 * column_share)
    extended = with_halo(kv_local, (("seq", 0),), per_shard)
    own_lists = lax.dynamic_slice_in_dim(neighbours, shard_index * per_shard, per_shard, 0)
    near_index = own_lists[:, : 1 + NEAR] - (shard_index - 1) * per_shard
    near_rows = extended[near_index]
    ref_count = per_shard * FAR
    far_lists = neighbours[:, 1 + NEAR :].reshape(seq_count, ref_count)
    owners = far_lists // per_shard
    local_ids = far_lists % per_shard
    earlier = jnp.arange(ref_count)[None, :] < jnp.arange(ref_count)[:, None]
    same_owner = owners[:, :, None] == owners[:, None, :]
    slot_ranks = jnp.sum(same_owner & earlier[None], axis=2)
    slot_count = (FAR * per_shard + seq_count - 2) // (seq_count - 1)
    owned_refs = (owners == shard_index).astype(jnp.float32)
    slot_hot = (slot_ranks[:, :, None] == jnp.arange(slot_count)[None, None, :]).astype(jnp.float32)
    local_hot = (local_ids[:, :, None] == jnp.arange(per_shard)[None, None, :]).astype(jnp.float32)
    selector = jnp.einsum("rk,rkj,rkl->rjl", owned_refs, slot_hot, local_hot).astype(jnp.bfloat16)
    flat_kv = kv_local.reshape(per_shard, PATCH * 2 * column_share)
    outgoing = jnp.dot(
        selector.reshape(seq_count * slot_count, per_shard),
        flat_kv,
        preferred_element_type=jnp.float32,
    )
    outgoing = outgoing.astype(jnp.bfloat16).reshape(seq_count, slot_count, PATCH, 2 * column_share)
    incoming = lax.all_to_all(outgoing, "seq", split_axis=0, concat_axis=0, tiled=True)
    my_owners = lax.dynamic_index_in_dim(owners, shard_index, 0, keepdims=False)
    my_slots = lax.dynamic_index_in_dim(slot_ranks, shard_index, 0, keepdims=False)
    far_rows = incoming.reshape(seq_count * slot_count, PATCH, 2 * column_share)[
        my_owners * slot_count + my_slots
    ]
    far_rows = far_rows.reshape(per_shard, FAR, PATCH, 2 * column_share)
    gathered = jnp.concatenate([near_rows, far_rows], axis=1).reshape(
        per_shard, NEIGH * PATCH, 2 * column_share
    )
    attended = lax.map(
        attend_patch, (queries.reshape(per_shard, PATCH, column_share), gathered)
    ).reshape(row_count, column_share)
    owned_rows = lax.all_to_all(attended, "head", split_axis=0, concat_axis=1, tiled=True)
    update = jnp.dot(owned_rows, out_weight, preferred_element_type=jnp.float32).astype(
        jnp.bfloat16
    )
    return update


def solution(mesh):
    placed = (P(("seq", "head"), None), P(), P(), P(), P())
    return jax.shard_map(
        body, mesh=mesh, in_specs=placed, out_specs=P(("seq", "head"), None), check_vma=False
    )
```

profile of v0, /device:TPU:16, one launch (start us, length us, event | category | flops | bytes accessed | tf_op | source)
XLA Modules:
  0.0 306.8 jit_solution(17444510389994302412)
XLA Ops:
  7.8 2.0 fusion.12
  14.0 18.4 %all-gather.2.cloned.1.call-done = bf16[1024,512]{1,0:T(8,128)(2,1)} async-done(((bf16[512,512]{1,0:T(8,128)(2,1)}), bf16[1024,512]{1,0:T(8,128)(2,1)}) %all-gather.2.cloned.1.call-update) | async-done | bytes 1048592 | tf_op jit(solution)/shard_map/all_gather | solution.py:65
  32.4 2.5 convolution_convert_fusion.1
  38.2 3.5 %copy.78 = bf16[2,8,256,512]{3,2,1,0:T(8,128)(2,1)} copy(bf16[2,8,256,512]{3,1,2,0:T(8,128)(2,1)S(1)} %bitcast.71) | data formatting | bytes 8388608
  41.7 6.0 %all-to-all-start = ((bf16[16,1,256,512]{3,2,1,0:T(8,128)(2,1)}), bf16[16,1,256,512]{3,2,1,0:T(8,128)(2,1)}, u32[]{:S(2)}, u32[]{:S(2)}) async-start(bf16[16,1,256,512]{3,2,1,0:T(8,128)(2,1)} %bitcast.72), calls=%async_computation | async-start | bytes 8388608 | tf_op jit(solution)/shard_map/all_to_all | solution.py:96
  49.8 4.6 %collective-permute-start.1 = (bf16[4,256,512]{2,1,0:T(8,128)(2,1)S(1)}, bf16[4,256,512]{2,1,0:T(8,128)(2,1)}, u32[]{:S(2)}, u32[]{:S(2)}) collective-permute-start(bf16[4,256,512]{2,1,0:T(8,128)(2,1)S(1)} %bitcast.75), channel_id=1, source_target_pairs={{2,0},{4,2},{6,4},{8,6},{10,8},{12,10},{14,12},{16,14},{18,16},{20... | collective-permute-start | bytes 3145736 | tf_op jit(solution)/shard_map/ppermute | solution.py:25
  54.9 96.6 %collective-permute-done = bf16[4,256,512]{2,1,0:T(8,128)(2,1)S(1)} collective-permute-done((bf16[4,256,512]{2,1,0:T(8,128)(2,1)S(1)}, bf16[4,256,512]{2,1,0:T(8,128)(2,1)S(1)}, u32[]{:S(2)}, u32[]{:S(2)}) %collective-permute-start) | collective-permute-done | bytes 1048608 | tf_op jit(solution)/shard_map/ppermute | solution.py:23
  151.6 2.8 pad_maximum_fusion.1
  154.4 6.1 %gather_fusion = bf16[20,256,512]{2,1,0:T(8,128)(2,1)} fusion(bf16[12,256,512]{2,1,0:T(8,128)(2,1)} %pad_maximum_fusion.1, s32[1024]{0:T(1024)S(1)} %pad_clamp_fusion.1), kind=kCustom, calls=%fused_computation | custom fusion | bytes 10485840 | tf_op jit(solution)/shard_map/gather | solution.py:76
  160.5 13.8 %copy.68 = bf16[4,5,256,512]{2,1,3,0:T(8,128)(2,1)} copy(bf16[4,5,256,512]{3,2,1,0:T(8,128)(2,1)} %bitcast.70) | data formatting | bytes 10485760 | tf_op jit(solution)/shard_map/gather | solution.py:76
  174.3 4.8 %gather_fusion.1 = bf16[12,256,512]{2,1,0:T(8,128)(2,1)} fusion(bf16[16,256,512]{2,1,0:T(8,128)(2,1)} %bitcast.16, s32[1024]{0:T(1024)S(1)} %pad_clamp_fusion), kind=kCustom, calls=%fused_computation.1 | custom fusion | bytes 6291504 | tf_op jit(solution)/shard_map/gather | solution.py:99
  179.1 7.1 %copy.69 = bf16[4,3,256,512]{2,1,3,0:T(4,128)(2,1)} copy(bf16[4,3,256,512]{3,2,1,0:T(8,128)(2,1)} %bitcast.73) | data formatting | bytes 6291456 | tf_op jit(solution)/shard_map/reshape | solution.py:102
  186.2 9.7 %pad_maximum_fusion = bf16[4,8,256,512]{2,1,3,0:T(8,128)(2,1)} fusion(bf16[4,3,256,512]{2,1,3,0:T(4,128)(2,1)} %copy.69, bf16[4,5,256,512]{2,1,3,0:T(8,128)(2,1)} %copy.68), kind=kLoop, calls=%fused_computation.16 | loop fusion | flops 16777216 | bytes 16777216 | tf_op jit(solution)/shard_map/concatenate | solution.py:103
  196.0 13.5 %reshape.188 = bf16[4,2048,512]{1,2,0:T(8,128)(2,1)} reshape(bf16[4,8,256,512]{2,1,3,0:T(8,128)(2,1)} %pad_maximum_fusion) | data formatting | bytes 16777216 | tf_op jit(solution)/shard_map/reshape | solution.py:103
  209.5 79.0 %while.10 = (s32[]{:T(128)}, bf16[4,256,256]{2,1,0:T(8,128)(2,1)}, bf16[4,2048,512]{1,2,0:T(8,128)(2,1)}, bf16[4,256,256]{2,1,0:T(8,128)(2,1)S(1)}, s32[]{:T(128)}) while((s32[]{:T(128)}, bf16[4,256,256]{2,1,0:T(8,128)(2,1)}, bf16[4,2048,512]{1,2,0:T(8,128)(2,1)}, bf16[4,256,256]{2,1,0:T(8,128)(2,1)S(1)}, s32[]{:T(128)}) %tuple.36), condition=%wide.region_5.6_spmd, body=%wide.region_2.5_spmd.sunk | while | flops 557910016 | bytes 45367876 | solution.py:106
  211.5 8.5 %fusion.44 = (f32[8,256]{1,0:T(8,128)S(1)}, f32[8,256,2048]{2,1,0:T(8,128)}) fusion(bf16[256,8,32]{0,2,1:T(8,128)(2,1)S(1)} %bitcast.78, bf16[2048,8,32]{0,2,1:T(8,128)(2,1)S(1)} %bitcast.69), kind=kOutput, calls=%fused_computation.52.clone.1 | convolution fusion | flops 281020416 | bytes 17965056 | tf_op jit(solution)/shard_map/while/body/eval_jaxpr/sub | solution.py:43
  220.0 8.5 %fusion.45 = bf16[8,32,256]{2,1,0:T(8,128)(2,1)S(1)} fusion(bf16[2048,8,32]{0,2,1:T(8,128)(2,1)S(1)} %bitcast.68, f32[8,256,2048]{2,1,0:T(8,128)} %get-tuple-element.97, f32[8,256]{1,0:T(8,128)S(1)} %get-tuple-element.98), kind=kOutput, calls=%fused_computation.11.clone.1 | convolution fusion | flops 276889600 | bytes 17965056 | tf_op jit(solution)/shard_map/while/body/eval_jaxpr/hqk,khd->qhd/dot_general | solution.py:45
  231.2 8.5 %fusion.44 = (f32[8,256]{1,0:T(8,128)S(1)}, f32[8,256,2048]{2,1,0:T(8,128)}) fusion(bf16[256,8,32]{0,2,1:T(8,128)(2,1)S(1)} %bitcast.78, bf16[2048,8,32]{0,2,1:T(8,128)(2,1)S(1)} %bitcast.69), kind=kOutput, calls=%fused_computation.52.clone.1 | convolution fusion | flops 281020416 | bytes 17965056 | tf_op jit(solution)/shard_map/while/body/eval_jaxpr/sub | solution.py:43
  239.7 8.5 %fusion.45 = bf16[8,32,256]{2,1,0:T(8,128)(2,1)S(1)} fusion(bf16[2048,8,32]{0,2,1:T(8,128)(2,1)S(1)} %bitcast.68, f32[8,256,2048]{2,1,0:T(8,128)} %get-tuple-element.97, f32[8,256]{1,0:T(8,128)S(1)} %get-tuple-element.98), kind=kOutput, calls=%fused_computation.11.clone.1 | convolution fusion | flops 276889600 | bytes 17965056 | tf_op jit(solution)/shard_map/while/body/eval_jaxpr/hqk,khd->qhd/dot_general | solution.py:45
  251.0 8.5 %fusion.44 = (f32[8,256]{1,0:T(8,128)S(1)}, f32[8,256,2048]{2,1,0:T(8,128)}) fusion(bf16[256,8,32]{0,2,1:T(8,128)(2,1)S(1)} %bitcast.78, bf16[2048,8,32]{0,2,1:T(8,128)(2,1)S(1)} %bitcast.69), kind=kOutput, calls=%fused_computation.52.clone.1 | convolution fusion | flops 281020416 | bytes 17965056 | tf_op jit(solution)/shard_map/while/body/eval_jaxpr/sub | solution.py:43
  259.5 8.5 %fusion.45 = bf16[8,32,256]{2,1,0:T(8,128)(2,1)S(1)} fusion(bf16[2048,8,32]{0,2,1:T(8,128)(2,1)S(1)} %bitcast.68, f32[8,256,2048]{2,1,0:T(8,128)} %get-tuple-element.97, f32[8,256]{1,0:T(8,128)S(1)} %get-tuple-element.98), kind=kOutput, calls=%fused_computation.11.clone.1 | convolution fusion | flops 276889600 | bytes 17965056 | tf_op jit(solution)/shard_map/while/body/eval_jaxpr/hqk,khd->qhd/dot_general | solution.py:45
  270.7 8.5 %fusion.44 = (f32[8,256]{1,0:T(8,128)S(1)}, f32[8,256,2048]{2,1,0:T(8,128)}) fusion(bf16[256,8,32]{0,2,1:T(8,128)(2,1)S(1)} %bitcast.78, bf16[2048,8,32]{0,2,1:T(8,128)(2,1)S(1)} %bitcast.69), kind=kOutput, calls=%fused_computation.52.clone.1 | convolution fusion | flops 281020416 | bytes 17965056 | tf_op jit(solution)/shard_map/while/body/eval_jaxpr/sub | solution.py:43
  279.2 8.5 %fusion.45 = bf16[8,32,256]{2,1,0:T(8,128)(2,1)S(1)} fusion(bf16[2048,8,32]{0,2,1:T(8,128)(2,1)S(1)} %bitcast.68, f32[8,256,2048]{2,1,0:T(8,128)} %get-tuple-element.97, f32[8,256]{1,0:T(8,128)S(1)} %get-tuple-element.98), kind=kOutput, calls=%fused_computation.11.clone.1 | convolution fusion | flops 276889600 | bytes 17965056 | tf_op jit(solution)/shard_map/while/body/eval_jaxpr/hqk,khd->qhd/dot_general | solution.py:45
  288.5 10.1 %all_to_all.24 = bf16[2,512,256]{2,1,0:T(8,128)(2,1)S(1)} all-to-all(bf16[2,512,256]{2,1,0:T(8,128)(2,1)} %bitcast.83), channel_id=1, replica_groups=mesh['seq'=16,'head'=2] {'head'}, dimensions={0} | all-to-all | bytes 1048576 | tf_op jit(solution)/shard_map/all_to_all | solution.py:109
  (67 shorter events, 23.7 us)
Async XLA Ops:
  6.5 292.2 %copy-start = (bf16[512,512]{1,0:T(8,128)(2,1)S(1)}, bf16[512,512]{1,0:T(8,128)(2,1)}, u32[]{:S(2)}) copy-start(bf16[512,512]{1,0:T(8,128)(2,1)} %param.10) | copy-start | bytes 1572868
  6.5 6.4 %copy-start.2 = (s32[64,8]{0,1:T(8,128)S(1)}, s32[64,8]{0,1:T(8,128)}, u32[]{:S(2)}) copy-start(s32[64,8]{0,1:T(8,128)} %param.11) | copy-start | bytes 6148
  6.5 25.9 %all-gather.2.cloned.1.call-start = ((), (), s32[]{:S(2)}) async-start(), calls=%async_computation.2 | async-start | bytes 1572864 | tf_op jit(solution)/shard_map/all_gather | solution.py:65
  34.9 1.2 copy-start.1
  41.7 132.6 %all-to-all-start = ((bf16[16,1,256,512]{3,2,1,0:T(8,128)(2,1)}), bf16[16,1,256,512]{3,2,1,0:T(8,128)(2,1)}, u32[]{:S(2)}, u32[]{:S(2)}) async-start(bf16[16,1,256,512]{3,2,1,0:T(8,128)(2,1)} %bitcast.72), calls=%async_computation | async-start | bytes 8388608 | tf_op jit(solution)/shard_map/all_to_all | solution.py:96
  47.8 103.8 %collective-permute-start = (bf16[4,256,512]{2,1,0:T(8,128)(2,1)S(1)}, bf16[4,256,512]{2,1,0:T(8,128)(2,1)S(1)}, u32[]{:S(2)}, u32[]{:S(2)}) collective-permute-start(bf16[4,256,512]{2,1,0:T(8,128)(2,1)S(1)} %bitcast.74), channel_id=1, source_target_pairs={{0,2},{2,4},{4,6},{6,8},{8,10},{10,12},{12,14},{14,16},{16,18},{18... | collective-permute-start | bytes 3145736 | tf_op jit(solution)/shard_map/ppermute | solution.py:23
  49.8 101.8 %collective-permute-start.1 = (bf16[4,256,512]{2,1,0:T(8,128)(2,1)S(1)}, bf16[4,256,512]{2,1,0:T(8,128)(2,1)}, u32[]{:S(2)}, u32[]{:S(2)}) collective-permute-start(bf16[4,256,512]{2,1,0:T(8,128)(2,1)S(1)} %bitcast.75), channel_id=1, source_target_pairs={{2,0},{4,2},{6,4},{8,6},{10,8},{12,10},{14,12},{16,14},{18,16},{20... | collective-permute-start | bytes 3145736 | tf_op jit(solution)/shard_map/ppermute | solution.py:25
  196.0 13.5 %slice-start = ((bf16[1024,768]{1,0:T(8,128)(2,1)}), bf16[1024,256]{1,0:T(8,128)(2,1)S(1)}, s32[]{:S(2)}) async-start(bf16[1024,768]{1,0:T(8,128)(2,1)} %copy-done.1), calls=%async_computation.3 | async-start | bytes 1048576 | tf_op jit(solution)/shard_map/slice | solution.py:71
Sparse Core Ops, SparseCore 0:
  10.0 22.3 all-gather.1
where the time goes:
time: 308 us; the launch traced here: 307 us
  waiting for transfers between devices  115 us (37%)
  matrix products  72.9 us (24%)
  local copies, waits for them, and re-layouts  66 us (21%)
  other arithmetic  16.5 us (5%)
  between operations  13.5 us (4%)
  starting transfers between devices  12.7 us (4%)
  blocking collectives  10.1 us (3%)
    ppermute x1, waiting for transfers between devices, with_halo(): lax.ppermute(tail, axis, [(i, (i + 1) % count) for i in range(ends)])  96.6 us
    sub x4, matrix products, attend_patch(): lifted = jnp.exp(scores - row_top)  33.9 us
    dot_general x4, matrix products, attend_patch(): jnp.einsum('hqk,khd->qhd', weights, values, preferred_element_type=jnp.fl...  33.8 us
    gather x2, local copies, waits for them, and re-layouts, body(): near_rows = extended[near_index]  19.9 us
    all_gather x1, waiting for transfers between devices, body(): lax.all_gather(normed, 'head', axis=0, tiled=True)  18.4 us
    reshape x1, local copies, waits for them, and re-layouts, body(): jnp.concatenate([near_rows, far_rows], axis=1)  13.5 us
    all_to_all x1, blocking collectives, body(): lax.all_to_all(attended, 'head', split_axis=0, concat_axis=1, tiled=True)  10.1 us
    concatenate x1, other arithmetic, body(): jnp.concatenate([near_rows, far_rows], axis=1)  9.73 us
  transfers between devices with their start and end apart: 4, of which 2 were waited for; matrix products, arithmetic and copies ran while one was open for 9% of the time, Pallas kernels for 0%

commit v1 on v0

--- a/solution.py
+++ b/solution.py
@@ -10,6 +10,28 @@
 NEAR = 4
 FAR = 3
 EPS = 1e-06
+
+
+def laid_out(blocks, dim):
+    shape = list(blocks.shape[1:])
+    shape[dim] *= blocks.shape[0]
+    return jnp.moveaxis(blocks, 0, dim).reshape(shape)
+
+
+def doubled(x, axis):
+    size = lax.axis_size(axis)
+    blocks = x[None]
+    for level in range(size.bit_length() - 1):
+        apart = 1 << level
+        other = lax.ppermute(blocks, axis, [(i, i ^ apart) for i in range(size)])
+        both = jnp.stack([blocks, other])
+        upper = lax.axis_index(axis) >> level & 1
+        blocks = jnp.where(upper == 0, both, both[::-1]).reshape(-1, *x.shape)
+    return blocks
+
+
+def doubled_up(x, axis, dim):
+    return laid_out(doubled(x, axis), dim)
 
 
 def with_halo(cells, sides, width):
@@ -62,9 +84,7 @@
     )
     own_columns = lax.dynamic_index_in_dim(grouped_weight, head_index, 1, keepdims=False)
     projected = jnp.dot(
-        lax.all_gather(normed, "head", axis=0, tiled=True),
-        own_columns,
-        preferred_element_type=jnp.float32,
+        doubled_up(normed, "head", 0), own_columns, preferred_element_type=jnp.float32
     ).astype(jnp.bfloat16)
     row_count = projected.shape[0]
     per_shard = row_count // PATCH

time: 308 us -> 287 us (0.932)
  between operations: 13.5 us -> 0.17 us
  waiting for transfers between devices: 115 us -> 105 us
    all_gather x1 -> x0, waiting for transfers between devices: 18.4 us -> none  [body(): lax.all_gather(normed, 'head', axis=0, tiled=True)]
    ppermute x0 -> x1, waiting for transfers between devices: none -> 8.12 us  [doubled(): other = lax.ppermute(blocks, axis, [(i, i ^ apart) for i in range(size)])]
  transfers between devices with their start and end apart: 4 -> 4, of which waited for: 2 -> 2; matrix products, arithmetic and copies ran while one was open for 9% -> 10% of each run, Pallas kernels for 0% -> 0%
where the time goes in v1:
time: 287 us; the launch traced here: 285 us
  waiting for transfers between devices  105 us (37%)
  matrix products  72.6 us (25%)
  local copies, waits for them, and re-layouts  66.1 us (23%)
  other arithmetic  17 us (6%)
  starting transfers between devices  14.4 us (5%)
  blocking collectives  10.1 us (4%)
    ppermute x1, waiting for transfers between devices, with_halo(): lax.ppermute(tail, axis, [(i, (i + 1) % count) for i in range(ends)])  96.6 us
    sub x4, matrix products, attend_patch(): lifted = jnp.exp(scores - row_top)  33.9 us
    dot_general x4, matrix products, attend_patch(): jnp.einsum('hqk,khd->qhd', weights, values, preferred_element_type=jnp.fl...  33.8 us
    gather x2, local copies, waits for them, and re-layouts, body(): near_rows = extended[near_index]  19.9 us
    reshape x1, local copies, waits for them, and re-layouts, body(): jnp.concatenate([near_rows, far_rows], axis=1)  13.5 us
    all_to_all x1, blocking collectives, body(): lax.all_to_all(attended, 'head', split_axis=0, concat_axis=1, tiled=True)  10.1 us
    concatenate x1, other arithmetic, body(): jnp.concatenate([near_rows, far_rows], axis=1)  9.73 us
    ppermute x1, waiting for transfers between devices, doubled(): other = lax.ppermute(blocks, axis, [(i, i ^ apart) for i in range(size)])  8.12 us
  transfers between devices with their start and end apart: 4, of which 2 were waited for; matrix products, arithmetic and copies ran while one was open for 10% of the time, Pallas kernels for 0%

profile of v1, /device:TPU:16, one launch (start us, length us, event | category | flops | bytes accessed | tf_op | source)
XLA Modules:
  0.0 285.2 jit_solution(1511712126649864077)
XLA Ops:
  8.3 8.1 %collective-permute-done = bf16[1,512,512]{2,1,0:T(8,128)(2,1)} collective-permute-done((bf16[1,512,512]{2,1,0:T(8,128)(2,1)S(1)}, bf16[1,512,512]{2,1,0:T(8,128)(2,1)}, u32[]{:S(2)}, u32[]{:S(2)}) %collective-permute-start) | collective-permute-done | bytes 524320 | tf_op jit(solution)/shard_map/ppermute | solution.py:26
  17.7 2.2 convolution_convert_fusion.1
  23.2 3.5 %copy.78 = bf16[2,8,256,512]{3,2,1,0:T(8,128)(2,1)} copy(bf16[2,8,256,512]{3,1,2,0:T(8,128)(2,1)S(1)} %bitcast.77) | data formatting | bytes 8388608
  26.7 6.2 %all-to-all-start = ((bf16[16,1,256,512]{3,2,1,0:T(8,128)(2,1)}), bf16[16,1,256,512]{3,2,1,0:T(8,128)(2,1)}, u32[]{:S(2)}, u32[]{:S(2)}) async-start(bf16[16,1,256,512]{3,2,1,0:T(8,128)(2,1)} %bitcast.78), calls=%async_computation | async-start | bytes 8388608 | tf_op jit(solution)/shard_map/all_to_all | solution.py:116
  32.9 2.0 collective-permute-start.1
  34.9 4.6 %collective-permute-start.2 = (bf16[4,256,512]{2,1,0:T(8,128)(2,1)S(1)}, bf16[4,256,512]{2,1,0:T(8,128)(2,1)}, u32[]{:S(2)}, u32[]{:S(2)}) collective-permute-start(bf16[4,256,512]{2,1,0:T(8,128)(2,1)S(1)} %bitcast.81), channel_id=1, source_target_pairs={{2,0},{4,2},{6,4},{8,6},{10,8},{12,10},{14,12},{16,14},{18,16},{20... | collective-permute-start | bytes 3145736 | tf_op jit(solution)/shard_map/ppermute | solution.py:47
  40.1 96.6 %collective-permute-done.1 = bf16[4,256,512]{2,1,0:T(8,128)(2,1)S(1)} collective-permute-done((bf16[4,256,512]{2,1,0:T(8,128)(2,1)S(1)}, bf16[4,256,512]{2,1,0:T(8,128)(2,1)S(1)}, u32[]{:S(2)}, u32[]{:S(2)}) %collective-permute-start.1) | collective-permute-done | bytes 1048608 | tf_op jit(solution)/shard_map/ppermute | solution.py:45
  136.7 2.8 pad_maximum_fusion.1
  139.5 6.1 %gather_fusion = bf16[20,256,512]{2,1,0:T(8,128)(2,1)} fusion(bf16[12,256,512]{2,1,0:T(8,128)(2,1)} %pad_maximum_fusion.1, s32[1024]{0:T(1024)S(1)} %pad_clamp_fusion.1), kind=kCustom, calls=%fused_computation | custom fusion | bytes 10485840 | tf_op jit(solution)/shard_map/gather | solution.py:96
  145.6 13.8 %copy.68 = bf16[4,5,256,512]{2,1,3,0:T(8,128)(2,1)} copy(bf16[4,5,256,512]{3,2,1,0:T(8,128)(2,1)} %bitcast.76) | data formatting | bytes 10485760 | tf_op jit(solution)/shard_map/gather | solution.py:96
  159.4 4.8 %gather_fusion.1 = bf16[12,256,512]{2,1,0:T(8,128)(2,1)} fusion(bf16[16,256,512]{2,1,0:T(8,128)(2,1)} %bitcast.20, s32[1024]{0:T(1024)S(1)} %pad_clamp_fusion), kind=kCustom, calls=%fused_computation.1 | custom fusion | bytes 6291504 | tf_op jit(solution)/shard_map/gather | solution.py:119
  164.3 7.1 %copy.69 = bf16[4,3,256,512]{2,1,3,0:T(4,128)(2,1)} copy(bf16[4,3,256,512]{3,2,1,0:T(8,128)(2,1)} %bitcast.79) | data formatting | bytes 6291456 | tf_op jit(solution)/shard_map/reshape | solution.py:122
  171.4 9.7 %pad_maximum_fusion = bf16[4,8,256,512]{2,1,3,0:T(8,128)(2,1)} fusion(bf16[4,3,256,512]{2,1,3,0:T(4,128)(2,1)} %copy.69, bf16[4,5,256,512]{2,1,3,0:T(8,128)(2,1)} %copy.68), kind=kLoop, calls=%fused_computation.16 | loop fusion | flops 16777216 | bytes 16777216 | tf_op jit(solution)/shard_map/concatenate | solution.py:123
  181.1 13.5 %reshape.188 = bf16[4,2048,512]{1,2,0:T(8,128)(2,1)} reshape(bf16[4,8,256,512]{2,1,3,0:T(8,128)(2,1)} %pad_maximum_fusion) | data formatting | bytes 16777216 | tf_op jit(solution)/shard_map/reshape | solution.py:123
  194.7 79.0 %while.10 = (s32[]{:T(128)}, bf16[4,256,256]{2,1,0:T(8,128)(2,1)}, bf16[4,2048,512]{1,2,0:T(8,128)(2,1)}, bf16[4,256,256]{2,1,0:T(8,128)(2,1)S(1)}, s32[]{:T(128)}) while((s32[]{:T(128)}, bf16[4,256,256]{2,1,0:T(8,128)(2,1)}, bf16[4,2048,512]{1,2,0:T(8,128)(2,1)}, bf16[4,256,256]{2,1,0:T(8,128)(2,1)S(1)}, s32[]{:T(128)}) %tuple.35), condition=%wide.region_5.6_spmd, body=%wide.region_2.5_spmd.sunk | while | flops 557910016 | bytes 45367876 | solution.py:126
  196.7 8.5 %fusion.46 = (f32[8,256]{1,0:T(8,128)S(1)}, f32[8,256,2048]{2,1,0:T(8,128)}) fusion(bf16[256,8,32]{0,2,1:T(8,128)(2,1)S(1)} %bitcast.84, bf16[2048,8,32]{0,2,1:T(8,128)(2,1)S(1)} %bitcast.75), kind=kOutput, calls=%fused_computation.56.clone.1 | convolution fusion | flops 281020416 | bytes 17965056 | tf_op jit(solution)/shard_map/while/body/eval_jaxpr/sub | solution.py:65
  205.2 8.5 %fusion.47 = bf16[8,32,256]{2,1,0:T(8,128)(2,1)S(1)} fusion(bf16[2048,8,32]{0,2,1:T(8,128)(2,1)S(1)} %bitcast.74, f32[8,256,2048]{2,1,0:T(8,128)} %get-tuple-element.99, f32[8,256]{1,0:T(8,128)S(1)} %get-tuple-element.100), kind=kOutput, calls=%fused_computation.11.clone.1 | convolution fusion | flops 276889600 | bytes 17965056 | tf_op jit(solution)/shard_map/while/body/eval_jaxpr/hqk,khd->qhd/dot_general | solution.py:67
  216.4 8.5 %fusion.46 = (f32[8,256]{1,0:T(8,128)S(1)}, f32[8,256,2048]{2,1,0:T(8,128)}) fusion(bf16[256,8,32]{0,2,1:T(8,128)(2,1)S(1)} %bitcast.84, bf16[2048,8,32]{0,2,1:T(8,128)(2,1)S(1)} %bitcast.75), kind=kOutput, calls=%fused_computation.56.clone.1 | convolution fusion | flops 281020416 | bytes 17965056 | tf_op jit(solution)/shard_map/while/body/eval_jaxpr/sub | solution.py:65
  224.9 8.5 %fusion.47 = bf16[8,32,256]{2,1,0:T(8,128)(2,1)S(1)} fusion(bf16[2048,8,32]{0,2,1:T(8,128)(2,1)S(1)} %bitcast.74, f32[8,256,2048]{2,1,0:T(8,128)} %get-tuple-element.99, f32[8,256]{1,0:T(8,128)S(1)} %get-tuple-element.100), kind=kOutput, calls=%fused_computation.11.clone.1 | convolution fusion | flops 276889600 | bytes 17965056 | tf_op jit(solution)/shard_map/while/body/eval_jaxpr/hqk,khd->qhd/dot_general | solution.py:67
  236.2 8.5 %fusion.46 = (f32[8,256]{1,0:T(8,128)S(1)}, f32[8,256,2048]{2,1,0:T(8,128)}) fusion(bf16[256,8,32]{0,2,1:T(8,128)(2,1)S(1)} %bitcast.84, bf16[2048,8,32]{0,2,1:T(8,128)(2,1)S(1)} %bitcast.75), kind=kOutput, calls=%fused_computation.56.clone.1 | convolution fusion | flops 281020416 | bytes 17965056 | tf_op jit(solution)/shard_map/while/body/eval_jaxpr/sub | solution.py:65
  244.7 8.5 %fusion.47 = bf16[8,32,256]{2,1,0:T(8,128)(2,1)S(1)} fusion(bf16[2048,8,32]{0,2,1:T(8,128)(2,1)S(1)} %bitcast.74, f32[8,256,2048]{2,1,0:T(8,128)} %get-tuple-element.99, f32[8,256]{1,0:T(8,128)S(1)} %get-tuple-element.100), kind=kOutput, calls=%fused_computation.11.clone.1 | convolution fusion | flops 276889600 | bytes 17965056 | tf_op jit(solution)/shard_map/while/body/eval_jaxpr/hqk,khd->qhd/dot_general | solution.py:67
  255.9 8.5 %fusion.46 = (f32[8,256]{1,0:T(8,128)S(1)}, f32[8,256,2048]{2,1,0:T(8,128)}) fusion(bf16[256,8,32]{0,2,1:T(8,128)(2,1)S(1)} %bitcast.84, bf16[2048,8,32]{0,2,1:T(8,128)(2,1)S(1)} %bitcast.75), kind=kOutput, calls=%fused_computation.56.clone.1 | convolution fusion | flops 281020416 | bytes 17965056 | tf_op jit(solution)/shard_map/while/body/eval_jaxpr/sub | solution.py:65
  264.4 8.5 %fusion.47 = bf16[8,32,256]{2,1,0:T(8,128)(2,1)S(1)} fusion(bf16[2048,8,32]{0,2,1:T(8,128)(2,1)S(1)} %bitcast.74, f32[8,256,2048]{2,1,0:T(8,128)} %get-tuple-element.99, f32[8,256]{1,0:T(8,128)S(1)} %get-tuple-element.100), kind=kOutput, calls=%fused_computation.11.clone.1 | convolution fusion | flops 276889600 | bytes 17965056 | tf_op jit(solution)/shard_map/while/body/eval_jaxpr/hqk,khd->qhd/dot_general | solution.py:67
  273.6 10.1 %all_to_all.24 = bf16[2,512,256]{2,1,0:T(8,128)(2,1)S(1)} all-to-all(bf16[2,512,256]{2,1,0:T(8,128)(2,1)} %bitcast.90), channel_id=1, replica_groups=mesh['seq'=16,'head'=2] {'head'}, dimensions={0} | all-to-all | bytes 1048576 | tf_op jit(solution)/shard_map/all_to_all | solution.py:129
  (68 shorter events, 25.9 us)
Async XLA Ops:
  0.0 283.9 %copy-start = (bf16[512,512]{1,0:T(8,128)(2,1)S(1)}, bf16[512,512]{1,0:T(8,128)(2,1)}, u32[]{:S(2)}) copy-start(bf16[512,512]{1,0:T(8,128)(2,1)} %param.10) | copy-start | bytes 1572868
  0.0 7.1 %copy-start.2 = (s32[64,8]{0,1:T(8,128)S(1)}, s32[64,8]{0,1:T(8,128)}, u32[]{:S(2)}) copy-start(s32[64,8]{0,1:T(8,128)} %param.11) | copy-start | bytes 6148
  2.6 13.8 %collective-permute-start = (bf16[1,512,512]{2,1,0:T(8,128)(2,1)S(1)}, bf16[1,512,512]{2,1,0:T(8,128)(2,1)}, u32[]{:S(2)}, u32[]{:S(2)}) collective-permute-start(bf16[1,512,512]{2,1,0:T(8,128)(2,1)S(1)} %get-tuple-element.65), channel_id=1, source_target_pairs={{0,1},{1,0},{2,3},{3,2},{4,5},{5,4},{6,7},{7,6},{8,9},{9,8},{10,11... | collective-permute-start | bytes 1572872 | tf_op jit(solution)/shard_map/ppermute | solution.py:26
  19.9 1.2 copy-start.1
  26.7 132.7 %all-to-all-start = ((bf16[16,1,256,512]{3,2,1,0:T(8,128)(2,1)}), bf16[16,1,256,512]{3,2,1,0:T(8,128)(2,1)}, u32[]{:S(2)}, u32[]{:S(2)}) async-start(bf16[16,1,256,512]{3,2,1,0:T(8,128)(2,1)} %bitcast.78), calls=%async_computation | async-start | bytes 8388608 | tf_op jit(solution)/shard_map/all_to_all | solution.py:116
  32.9 103.8 %collective-permute-start.1 = (bf16[4,256,512]{2,1,0:T(8,128)(2,1)S(1)}, bf16[4,256,512]{2,1,0:T(8,128)(2,1)S(1)}, u32[]{:S(2)}, u32[]{:S(2)}) collective-permute-start(bf16[4,256,512]{2,1,0:T(8,128)(2,1)S(1)} %bitcast.80), channel_id=1, source_target_pairs={{0,2},{2,4},{4,6},{6,8},{8,10},{10,12},{12,14},{14,16},{16,18},{18... | collective-permute-start | bytes 3145736 | tf_op jit(solution)/shard_map/ppermute | solution.py:45
  34.9 101.8 %collective-permute-start.2 = (bf16[4,256,512]{2,1,0:T(8,128)(2,1)S(1)}, bf16[4,256,512]{2,1,0:T(8,128)(2,1)}, u32[]{:S(2)}, u32[]{:S(2)}) collective-permute-start(bf16[4,256,512]{2,1,0:T(8,128)(2,1)S(1)} %bitcast.81), channel_id=1, source_target_pairs={{2,0},{4,2},{6,4},{8,6},{10,8},{12,10},{14,12},{16,14},{18,16},{20... | collective-permute-start | bytes 3145736 | tf_op jit(solution)/shard_map/ppermute | solution.py:47
  181.1 13.5 %slice-start = ((bf16[1024,768]{1,0:T(8,128)(2,1)}), bf16[1024,256]{1,0:T(8,128)(2,1)S(1)}, s32[]{:S(2)}) async-start(bf16[1024,768]{1,0:T(8,128)(2,1)} %copy-done.1), calls=%async_computation.2 | async-start | bytes 1048576 | tf_op jit(solution)/shard_map/slice | solution.py:91
